TPU v7x, 256 devices: a whole 4x4x8 slice. The times are simulated.
256 devices in a mesh: blk: 16 (over z, x_hi), leaf: 8 (over y, core), rhs: 2 (over x_lo).
Axes of the slice: x: 4 (x_hi: 2, x_lo: 2; x = x_hi * 2 + x_lo), y: 4, z: 8, core: 2. Of those that a mesh axis runs over, the one named last changes fastest.
Arguments:
- residual: float32 [32, 8, 65536], P('rhs', 'leaf', 'blk'), may hold values from -160 to 160
- points: float32 [3, 8, 65536], P(None, 'leaf', 'blk'), may hold values from -12330 to 12330
- noise: float32 [8, 65536], P('leaf', 'blk'), may hold values from 1 to 2
- block_list: int32 [8, 8, 256], P('leaf'), may hold values from 0 to 1, as said below
Outputs:
- correction: float32 [32, 8, 65536], P('rhs', 'leaf', 'blk')
- new_residual: float32 [32, 8, 65536], P('rhs', 'leaf', 'blk')
- basis: float32 [128, 8, 65536], P('rhs', 'leaf', 'blk')
Inputs may be any that keep to these rules, and one draw needn't show every extreme that they name: The list is symmetric: block_list[t, k, i] == block_list[t, 7 - k, (i + d) mod 256] with d the offset of entry k.
All inputs are finite; a program needn't handle non-finite values.
Results may differ from a plain program's by a relative error of at most 0.007.
Values sent between devices are 32-bit elements; how exact they have to be, the bound alone decides.
A program may use at most 128 MiB of HBM per device.

v0:
```python
import jax
import jax.numpy as jnp
from jax import lax
from jax.sharding import PartitionSpec as P

M = 32
S = 4
BS = 256
REACH = 4
SUPPORT = 1408
centre_shift = 1.5
amplitude = 1.1
exact = lax.Precision.HIGHEST


def extended(x, sides, width):
    for axis, dim in sides:
        count, length = (lax.axis_size(axis), x.shape[dim])
        up = [(i, (i + 1) % count) for i in range(count)]
        down = [(j, i) for i, j in up]
        last = lax.slice_in_dim(x, length - width, length, axis=dim)
        leading = lax.slice_in_dim(x, 0, width, axis=dim)
        before = lax.ppermute(last, axis, up)
        after = lax.ppermute(leading, axis, down)
        x = jnp.concatenate([before, x, after], axis=dim)
    return x


def kernel_tile(near_points, own_points):
    squared = (near_points[0][:, None] - own_points[0][None, :]) ** 2
    squared = squared + (near_points[1][:, None] - own_points[1][None, :]) ** 2
    squared = squared + (near_points[2][:, None] - own_points[2][None, :]) ** 2
    radius = jnp.sqrt(squared) / SUPPORT
    remain = jnp.maximum(1.0 - radius, 0.0)
    return remain * remain * (remain * remain) * (4.0 * radius + 1.0) * (amplitude / SUPPORT)


def band_product(field_wide, points_wide, weights, rows_out):
    per_turn = rows_out // 8
    count = field_wide.shape[0]

    def turn(carry, index):
        pieces = []
        for inner in range(per_turn):
            block = index * per_turn + inner
            own_points = lax.dynamic_slice_in_dim(points_wide, (block + REACH) * BS, BS, 1)
            total = jnp.zeros((count, BS), jnp.float32)
            for offset in range(2 * REACH + 1):
                column_at = (block + offset) * BS
                near_points = lax.dynamic_slice_in_dim(points_wide, column_at, BS, 1)
                near_field = lax.dynamic_slice_in_dim(field_wide, column_at, BS, 1)
                listed = lax.dynamic_index_in_dim(weights[offset], block, 0, False)
                tile = kernel_tile(near_points, own_points) * listed
                total = total + jnp.dot(near_field, tile, precision=exact)
            pieces.append(total)
        return (carry, jnp.concatenate(pieces, axis=1))

    carry, parts = lax.scan(turn, jnp.zeros((), jnp.int32), jnp.arange(8, dtype=jnp.int32))
    return jnp.moveaxis(parts, 0, 1).reshape(count, rows_out * BS)


def galerkin(gram, count_points, count_sides):
    normed = gram / count_points
    basis_count = normed.shape[0] - count_sides
    gram_basis = normed[:basis_count, :basis_count]
    factor_low = jnp.linalg.cholesky(gram_basis)
    inverse_low = lax.linalg.triangular_solve(
        factor_low, jnp.eye(basis_count, dtype=jnp.float32), left_side=True, lower=True
    )
    cross = normed[:basis_count, count_sides:] + centre_shift * gram_basis
    projected = jnp.dot(
        jnp.dot(inverse_low, cross, precision=exact), inverse_low.T, precision=exact
    )
    projected = 0.5 * (projected + projected.T)
    small_side = jnp.dot(inverse_low, gram_basis[:, :count_sides], precision=exact)
    proj_factor = jnp.linalg.cholesky(projected)
    halfway = lax.linalg.triangular_solve(proj_factor, small_side, left_side=True, lower=True)
    coeffs = lax.linalg.triangular_solve(
        proj_factor, halfway, left_side=True, lower=True, transpose_a=True
    )
    combo = jnp.dot(coeffs.T, inverse_low, precision=exact)
    return (inverse_low, combo)


def row_products(rows):
    return lax.dot_general(rows, rows, (((1,), (1,)), ((), ())), precision=exact)


def local(residual, points, noise, block_list):
    field = residual[:, 0]
    coords = points[:, 0]
    nugget = noise[0]
    own_rows = field.shape[1]
    own_blocks = own_rows // BS
    first_block = lax.axis_index("blk") * own_blocks
    listed = block_list[0].astype(jnp.float32)
    nine = jnp.concatenate(
        [listed[:REACH], jnp.ones((1, listed.shape[1]), jnp.float32), listed[REACH:]], axis=0
    )
    margin = S * REACH
    wrapped = jnp.concatenate([nine[:, -margin:], nine, nine[:, :margin]], axis=1)
    powers = [field]
    rim = REACH * BS
    coords_wide = extended(coords, (("blk", 1),), rim)
    own_weights = lax.dynamic_slice_in_dim(wrapped, first_block + margin, own_blocks, 1)
    current = field
    for power_step in range(S):
        widened = extended(current, (("blk", 1),), rim)
        current = (
            band_product(widened, coords_wide, own_weights, own_blocks)
            + (nugget - centre_shift) * current
        )
        powers.append(current)
    half_panel = jnp.stack(powers, axis=0)
    count_points = own_rows * lax.axis_size("blk") * lax.axis_size("leaf")
    sides_here = field.shape[0]
    whole = lax.all_gather(half_panel, "rhs", axis=1, tiled=True)
    flat = whole.reshape(-1, own_rows)
    gram = lax.psum(row_products(flat), ("blk", "leaf"))
    inverse_low, combo = galerkin(gram, count_points, M)
    first_rows = flat[: S * M]
    image = flat[M:] + centre_shift * first_rows
    part = lax.axis_index("rhs")
    basis_here = S * M // lax.axis_size("rhs")
    mine_low = lax.dynamic_slice_in_dim(inverse_low, part * basis_here, basis_here, 0)
    mine_combo = lax.dynamic_slice_in_dim(combo, part * sides_here, sides_here, 0)
    correction = jnp.dot(mine_combo, first_rows, precision=exact)
    new_residual = field - jnp.dot(mine_combo, image, precision=exact)
    basis = jnp.dot(mine_low, first_rows, precision=exact)
    return (correction[:, None], new_residual[:, None], basis[:, None])


def solution(mesh):
    placed = (
        P("rhs", "leaf", "blk"),
        P(None, "leaf", "blk"),
        P("leaf", "blk"),
        P("leaf", None, None),
    )
    return jax.shard_map(
        local,
        mesh=mesh,
        in_specs=placed,
        out_specs=(P("rhs", "leaf", "blk"), P("rhs", "leaf", "blk"), P("rhs", "leaf", "blk")),
        check_vma=False,
    )
```

profile of v0, /device:TPU:2, one launch (start us, length us, event | category | flops | bytes accessed | tf_op | source)
XLA Modules:
  0.0 2114.2 jit_solution(17787421845742051918)
XLA Ops:
  8.1 2.2 collective-permute-start.2
  10.3 5.4 collective-permute-start.3
  16.9 5.6 collective-permute-start.1
  25.4 206.0 %while.52 = (s32[]{:T(128)}, f32[8,16,512]{2,1,0:T(8,128)S(1)}, s32[8]{0:T(128)S(1)}, f32[16,6144]{1,0:T(8,128)S(1)}, f32[3,6144]{1,0:T(4,128)S(1)}, /*index=5*/...) while((s32[]{:T(128)}, f32[8,16,512]{2,1,0:T(8,128)S(1)}, ...), condition=%wide.region_1.2_spmd, body=%wide.region_0.1_spmd.sunk | while | flops 246620224 | bytes 1092197 | solution.py:58
  231.9 5.6 collective-permute-start.5
  237.9 1.8 collective-permute-done.4
  239.8 202.8 %while.53 = (s32[]{:T(128)}, f32[8,16,512]{2,1,0:T(8,128)S(1)}, s32[8]{0:T(128)S(1)}, f32[16,6144]{1,0:T(8,128)S(1)}, f32[3,6144]{1,0:T(4,128)S(1)}, /*index=5*/...) while((s32[]{:T(128)}, f32[8,16,512]{2,1,0:T(8,128)S(1)}, ...), condition=%wide.region_3.4_spmd, body=%wide.region_2.3_spmd.sunk | while | flops 246620224 | bytes 1092197 | solution.py:58
  442.8 6.1 collective-permute-start.7
  449.2 1.5 collective-permute-done.6
  450.9 203.8 %while.54 = (s32[]{:T(128)}, f32[8,16,512]{2,1,0:T(8,128)S(1)}, s32[8]{0:T(128)S(1)}, f32[16,6144]{1,0:T(8,128)S(1)}, f32[3,6144]{1,0:T(4,128)S(1)}, /*index=5*/...) while((s32[]{:T(128)}, f32[8,16,512]{2,1,0:T(8,128)S(1)}, ...), condition=%wide.region_5.6_spmd, body=%wide.region_4.5_spmd.sunk | while | flops 246620224 | bytes 1092197 | solution.py:58
  654.8 1.9 collective-permute-start.8
  656.7 4.4 collective-permute-start.9
  661.4 1.8 collective-permute-done.8
  663.4 207.7 %while.55 = (s32[]{:T(128)}, f32[8,16,512]{2,1,0:T(8,128)S(1)}, s32[8]{0:T(128)S(1)}, f32[16,6144]{1,0:T(8,128)S(1)}, f32[3,6144]{1,0:T(4,128)S(1)}, /*index=5*/...) while((s32[]{:T(128)}, f32[8,16,512]{2,1,0:T(8,128)S(1)}, ...), condition=%wide.region_7.8_spmd, body=%wide.region_6.7_spmd.sunk | while | flops 246620224 | bytes 1092197 | solution.py:58
  872.7 45.1 %all-gather.2.cloned.1.call-done = f32[5,32,4096]{2,1,0:T(8,128)} async-done(((f32[5,16,4096]{2,1,0:T(8,128)}), f32[5,32,4096]{2,1,0:T(8,128)}) %all-gather.2.cloned.1.call-update) | async-done | bytes 2621456 | tf_op jit(solution)/shard_map/all_gather | solution.py:117
  917.8 5.6 fusion.2577
  925.2 1.6 bitcast_add_fusion
  926.8 1122.0 %all-reduce.2.cloned.1.call-done = f32[160,160]{0,1:T(8,128)} async-done(((f32[160,160]{0,1:T(8,128)}), f32[160,160]{0,1:T(8,128)}) %all-reduce.2.cloned.1.call-update) | async-done | bytes 102416 | tf_op jit(solution)/shard_map/psum | solution.py:119
  2049.9 11.7 cholesky.44
  2062.9 9.8 custom-call.10
  2074.0 12.0 cholesky.55
  2087.3 9.8 custom-call.11
  2097.8 2.7 fusion.2532
  2103.9 2.0 copy.30
  (960 shorter events, 433.6 us)
Async XLA Ops:
  7.2 910.6 %all-gather.2.cloned.1.call-start = ((), (), s32[]{:S(2)}) async-start(), calls=%async_computation | async-start | bytes 3932160 | tf_op jit(solution)/shard_map/all_gather | solution.py:117
  8.1 17.2 collective-permute-start.2
  10.3 15.0 collective-permute-start.3
  16.8 8.5 collective-permute-start
  16.9 8.4 collective-permute-start.1
  25.4 206.0 %copy-start.3 = (f32[16,1,4096]{2,1,0:T(1,128)S(1)}, f32[16,1,4096]{2,1,0:T(1,128)}, u32[]{:S(2)}) copy-start(f32[16,1,4096]{2,1,0:T(1,128)} %param.13) | copy-start | bytes 786436
  231.6 8.2 collective-permute-start.4
  231.9 7.9 collective-permute-start.5
  442.7 8.0 collective-permute-start.6
  442.8 8.0 collective-permute-start.7
  654.8 8.4 collective-permute-start.8
  656.7 6.6 collective-permute-start.9
  871.3 1.1 copy-start.4
  872.4 1176.4 %all-reduce.2.cloned.1.call-start = ((), (), s32[]{:S(2)}) async-start(), calls=%async_computation.1 | async-start | bytes 327680 | tf_op jit(solution)/shard_map/psum | solution.py:119
  917.8 5.6 copy-start
  923.9 1.3 copy-start.1
  2073.9 27.7 %copy-start.2 = (f32[4,32,4096]{2,1,0:T(8,128)S(1)}, f32[4,32,4096]{2,1,0:T(8,128)}, u32[]{:S(2)}) copy-start(f32[4,32,4096]{2,1,0:T(8,128)} %copy-done.1) | copy-start | bytes 6291460
Sparse Core Ops, SparseCore 0:
  872.5 45.1 all-gather.1
  923.5 1125.2 all-reduce.1
where the time goes:
time: 2130 us; the launch traced here: 2110 us
  waiting for transfers between devices  1170 us (55%)
  loops' own time  407 us (19%)
  matrix products  296 us (14%)
  local copies, waits for them, and re-layouts  140 us (7%)
  other arithmetic  51.7 us (2%)
  starting transfers between devices  32 us (2%)
    psum x1, waiting for transfers between devices, local(): gram = lax.psum(row_products(flat), ('blk', 'leaf'))  1120 us
    another operation x4, loops' own time, band_product(): lax.scan(turn, jnp.zeros((), jnp.int32), jnp.arange(8, dtype=jnp.int32))  407 us
    dot_general x576, matrix products, turn(): total = total + jnp.dot(near_field, tile, precision=exact)  284 us
    dynamic_slice x160, local copies, waits for them, and re-layouts, turn(): listed = lax.dynamic_index_in_dim(weights[offset], block, 0, False)  105 us
    all_gather x1, waiting for transfers between devices, local(): whole = lax.all_gather(half_panel, 'rhs', axis=1, tiled=True)  45.1 us
  transfers between devices with their start and end apart: 12, of which 7 were waited for; matrix products, arithmetic and copies ran while one was open for 0% of the time, Pallas kernels for 0%

commit v1 on v0

--- a/solution.py
+++ b/solution.py
@@ -114,7 +114,9 @@
     half_panel = jnp.stack(powers, axis=0)
     count_points = own_rows * lax.axis_size("blk") * lax.axis_size("leaf")
     sides_here = field.shape[0]
-    whole = lax.all_gather(half_panel, "rhs", axis=1, tiled=True)
+    whole = jnp.concatenate(
+        lax.all_to_all(jnp.stack([half_panel] * lax.axis_size("rhs")), "rhs", 0, 0), axis=1
+    )
     flat = whole.reshape(-1, own_rows)
     gram = lax.psum(row_products(flat), ("blk", "leaf"))
     inverse_low, combo = galerkin(gram, count_points, M)

time: 2130 us -> 2120 us (level)
    all_gather x1 -> x0, waiting for transfers between devices: 45.1 us -> none  [local(): whole = lax.all_gather(half_panel, 'rhs', axis=1, tiled=True)]
    all_to_all x0 -> x1, waiting for transfers between devices: none -> 24.5 us  [local(): lax.all_to_all(jnp.stack([half_panel] * lax.axis_size('rhs')), 'rhs', 0, 0)]
where the time goes in v1:
time: 2120 us; the launch traced here: 2110 us
  waiting for transfers between devices  1150 us (54%)
  loops' own time  414 us (20%)
  matrix products  293 us (14%)
  local copies, waits for them, and re-layouts  142 us (7%)
  other arithmetic  53.5 us (3%)
  starting transfers between devices  37.4 us (2%)
    psum x1, waiting for transfers between devices, local(): gram = lax.psum(row_products(flat), ('blk', 'leaf'))  1120 us
    another operation x4, loops' own time, band_product(): lax.scan(turn, jnp.zeros((), jnp.int32), jnp.arange(8, dtype=jnp.int32))  414 us
    dot_general x576, matrix products, turn(): total = total + jnp.dot(near_field, tile, precision=exact)  284 us
    dynamic_slice x160, local copies, waits for them, and re-layouts, turn(): listed = lax.dynamic_index_in_dim(weights[offset], block, 0, False)  105 us
  transfers between devices with their start and end apart: 12, of which 7 were waited for; matrix products, arithmetic and copies ran while one was open for 0% of the time, Pallas kernels for 0%

profile of v1, /device:TPU:2, one launch (start us, length us, event | category | flops | bytes accessed | tf_op | source)
XLA Modules:
  0.0 2106.4 jit_solution(8245058204112714715)
XLA Ops:
  8.0 2.2 collective-permute-start.2
  10.2 5.4 collective-permute-start.3
  16.8 5.6 collective-permute-start.1
  25.3 209.2 %while.52 = (s32[]{:T(128)}, f32[8,16,512]{2,1,0:T(8,128)S(1)}, s32[8]{0:T(128)S(1)}, f32[16,6144]{1,0:T(8,128)S(1)}, f32[3,6144]{1,0:T(4,128)S(1)}, /*index=5*/...) while((s32[]{:T(128)}, f32[8,16,512]{2,1,0:T(8,128)S(1)}, ...), condition=%wide.region_1.2_spmd, body=%wide.region_0.1_spmd.sunk | while | flops 246620224 | bytes 1092197 | solution.py:58
  234.8 5.9 collective-permute-start.5
  242.8 208.2 %while.53 = (s32[]{:T(128)}, f32[8,16,512]{2,1,0:T(8,128)S(1)}, s32[8]{0:T(128)S(1)}, f32[16,6144]{1,0:T(8,128)S(1)}, f32[3,6144]{1,0:T(4,128)S(1)}, /*index=5*/...) while((s32[]{:T(128)}, f32[8,16,512]{2,1,0:T(8,128)S(1)}, ...), condition=%wide.region_3.4_spmd, body=%wide.region_2.3_spmd.sunk | while | flops 246620224 | bytes 1092197 | solution.py:58
  451.2 6.4 collective-permute-start.7
  459.5 205.4 %while.54 = (s32[]{:T(128)}, f32[8,16,512]{2,1,0:T(8,128)S(1)}, s32[8]{0:T(128)S(1)}, f32[16,6144]{1,0:T(8,128)S(1)}, f32[3,6144]{1,0:T(4,128)S(1)}, /*index=5*/...) while((s32[]{:T(128)}, f32[8,16,512]{2,1,0:T(8,128)S(1)}, ...), condition=%wide.region_5.6_spmd, body=%wide.region_4.5_spmd.sunk | while | flops 246620224 | bytes 1092197 | solution.py:58
  665.0 1.8 collective-permute-start.8
  666.8 4.5 collective-permute-start.9
  671.6 1.8 collective-permute-done.8
  673.5 205.9 %while.55 = (s32[]{:T(128)}, f32[8,16,512]{2,1,0:T(8,128)S(1)}, s32[8]{0:T(128)S(1)}, f32[16,6144]{1,0:T(8,128)S(1)}, f32[3,6144]{1,0:T(4,128)S(1)}, /*index=5*/...) while((s32[]{:T(128)}, f32[8,16,512]{2,1,0:T(8,128)S(1)}, ...), condition=%wide.region_7.8_spmd, body=%wide.region_6.7_spmd.sunk | while | flops 246620224 | bytes 1092197 | solution.py:58
  879.7 1.7 pad_maximum_fusion
  881.4 5.1 all-to-all-start
  886.8 24.5 %all-to-all-done = f32[2,5,16,4096]{3,2,1,0:T(8,128)S(1)} async-done(((f32[2,5,16,4096]{3,2,1,0:T(8,128)}), f32[2,5,16,4096]{3,2,1,0:T(8,128)S(1)}, u32[]{:S(2)}, u32[]{:S(2)}) %all-to-all-start) | async-done | bytes 2621472 | tf_op jit(solution)/shard_map/all_to_all | solution.py:118
  911.5 2.6 fusion.2570
  914.1 2.9 fusion.2577
  920.4 1120.6 %all-reduce.2.cloned.1.call-done = f32[160,160]{0,1:T(8,128)} async-done(((f32[160,160]{0,1:T(8,128)}), f32[160,160]{0,1:T(8,128)}) %all-reduce.2.cloned.1.call-update) | async-done | bytes 102416 | tf_op jit(solution)/shard_map/psum | solution.py:121
  2042.1 11.7 cholesky.44
  2055.2 9.8 custom-call.10
  2066.2 12.0 cholesky.55
  2079.5 9.8 custom-call.11
  2090.1 2.7 fusion.2532
  2096.1 2.0 copy.33
  (959 shorter events, 437.9 us)
Async XLA Ops:
  8.0 17.2 collective-permute-start.2
  10.2 15.0 collective-permute-start.3
  16.7 8.5 collective-permute-start
  16.8 8.4 collective-permute-start.1
  25.3 209.2 %copy-start.2 = (f32[16,1,4096]{2,1,0:T(1,128)S(1)}, f32[16,1,4096]{2,1,0:T(1,128)}, u32[]{:S(2)}) copy-start(f32[16,1,4096]{2,1,0:T(1,128)} %param.13) | copy-start | bytes 786436
  234.7 8.0 collective-permute-start.4
  234.8 7.9 collective-permute-start.5
  451.1 8.2 collective-permute-start.6
  451.2 8.3 collective-permute-start.7
  665.0 8.4 collective-permute-start.8
  666.8 6.6 collective-permute-start.9
  881.4 29.8 %all-to-all-start = ((f32[2,5,16,4096]{3,2,1,0:T(8,128)}), f32[2,5,16,4096]{3,2,1,0:T(8,128)S(1)}, u32[]{:S(2)}, u32[]{:S(2)}) async-start(f32[2,5,16,4096]{3,2,1,0:T(8,128)} %pad_maximum_fusion), calls=%async_computation | async-start | bytes 5242880 | tf_op jit(solution)/shard_map/all_to_all | solution.py:118
  886.6 1154.5 %all-reduce.2.cloned.1.call-start = ((), (), s32[]{:S(2)}) async-start(), calls=%async_computation.1 | async-start | bytes 327680 | tf_op jit(solution)/shard_map/psum | solution.py:121
  914.1 2.9 copy-start.1
  917.0 1.6 copy-start
Sparse Core Ops, SparseCore 0:
  917.1 1123.8 all-reduce.1
